TPU v7x, 128 devices: a whole 4x4x4 slice. The times are simulated.
128 devices in a mesh: pos: 16 (over x, y), obj: 8 (over z, core).
Axes of the slice: x: 4, y: 4, z: 4, core: 2. Of those that a mesh axis runs over, the one named last changes fastest.
Arguments:
- object_field: float32 [2, 4096, 6144], P(None, 'obj', 'pos'), may hold values from -5 to 5
- probe: float32 [2, 256, 256], replicated, may hold values from -5 to 5
- amplitude: bfloat16 [2048, 256, 256], P(('pos', 'obj')), may hold values from 0.19921875 to 3
- row_offset: int32 [2048], P(('pos', 'obj')), may hold values from 0 to 256
- col_offset: int32 [2048], P(('pos', 'obj')), may hold values from 0 to 128
- owner: int32 [2048], P(('pos', 'obj')), may hold values from 0 to 15, as said below
Outputs:
- new_object: float32 [2, 4096, 6144], P(None, 'obj', 'pos')
- new_probe: float32 [2, 256, 256], replicated
Inputs may be any that keep to these rules, and one draw needn't show every extreme that they name: Among the 16 positions of one device no owner is named more than 2 times; in each row band one owner is named exactly 2 times by every device.
All inputs are finite; a program needn't handle non-finite values.
Results may differ from a plain program's by a relative error of at most 0.005.
The roundings to bfloat16 on the way count: a program that leaves them out, or rounds other values in their place, can miss the bound.
Values may be sent and summed in bfloat16 or wider, within the bound.
A program may use at most 128 MiB of HBM per device.

v0:
```python
import math
import jax
import jax.numpy as jnp
from jax import lax
from jax.sharding import PartitionSpec as P


def padded_2(block, sides, width):
    for axis, dim in sides:
        count = lax.axis_size(axis)
        forward = [(i, i + 1) for i in range(count - 1)]
        forward.append((count - 1, 0))
        backward = [(target, source) for source, target in forward]
        low = lax.ppermute(
            lax.slice_in_dim(block, block.shape[dim] - width, None, axis=dim), axis, forward
        )
        high = lax.ppermute(lax.slice_in_dim(block, 0, width, axis=dim), axis, backward)
        block = jnp.concatenate([low, block, high], axis=dim)
    return block


def dft_tables(size):
    index = jnp.arange(size, dtype=jnp.int32)
    product = index[:, None] * index[None, :] % size
    angle = product.astype(jnp.float32) * (2.0 * math.pi / size)
    scale = 1.0 / math.sqrt(size)
    real_part = (jnp.cos(angle) * scale).astype(jnp.bfloat16)
    imag_part = (-jnp.sin(angle) * scale).astype(jnp.bfloat16)
    return (real_part, imag_part)


def left_apply(mat_re, mat_im, val_re, val_im):

    def product(matrix, values):
        return jnp.einsum("jk,bkl->bjl", matrix, values, preferred_element_type=jnp.float32)

    return (
        product(mat_re, val_re) - product(mat_im, val_im),
        product(mat_re, val_im) + product(mat_im, val_re),
    )


def right_apply(val_re, val_im, mat_re, mat_im):

    def product(values, matrix):
        return jnp.einsum("bjk,kl->bjl", values, matrix, preferred_element_type=jnp.float32)

    return (
        product(val_re, mat_re) - product(val_im, mat_im),
        product(val_re, mat_im) + product(val_im, mat_re),
    )


def position_terms(patches, amps, validity, probe, tables):
    four_re, four_im, conj_im = tables
    patch_re = patches[:, 0].astype(jnp.float32)
    patch_im = patches[:, 1].astype(jnp.float32)
    probe_re = probe[0]
    probe_im = probe[1]
    psi_re = (probe_re * patch_re - probe_im * patch_im).astype(jnp.bfloat16)
    psi_im = (probe_re * patch_im + probe_im * patch_re).astype(jnp.bfloat16)
    left_re, left_im = left_apply(four_re, four_im, psi_re, psi_im)
    wave_re, wave_im = right_apply(
        left_re.astype(jnp.bfloat16), left_im.astype(jnp.bfloat16), four_re, four_im
    )
    magnitude = jnp.sqrt(wave_re * wave_re + wave_im * wave_im)
    factor = 1.0 - amps.astype(jnp.float32) / jnp.maximum(magnitude, 0.5)
    diff_re = (wave_re * factor).astype(jnp.bfloat16)
    diff_im = (wave_im * factor).astype(jnp.bfloat16)
    back_re, back_im = left_apply(four_re, conj_im, diff_re, diff_im)
    chi_re, chi_im = right_apply(
        back_re.astype(jnp.bfloat16), back_im.astype(jnp.bfloat16), four_re, conj_im
    )
    chi_re = chi_re * validity[:, None, None]
    chi_im = chi_im * validity[:, None, None]
    grad_re = (probe_re * chi_re + probe_im * chi_im).astype(jnp.bfloat16)
    grad_im = (probe_re * chi_im - probe_im * chi_re).astype(jnp.bfloat16)
    term_re = jnp.sum(patch_re * chi_re + patch_im * chi_im, axis=0)
    term_im = jnp.sum(patch_re * chi_im - patch_im * chi_re, axis=0)
    return (jnp.stack([grad_re, grad_im], axis=1), jnp.stack([term_re, term_im]))


def run_terms(patches, amps, validity, probe, tables):
    count = patches.shape[0]
    size = patches.shape[2]
    batch_size = math.gcd(count, 8)
    groups = count // batch_size
    grouped = (
        patches.reshape(groups, batch_size, 2, size, size),
        amps.reshape(groups, batch_size, size, size),
        validity.reshape(groups, batch_size),
    )
    grads, terms = lax.map(
        lambda items: position_terms(items[0], items[1], items[2], probe, tables), grouped
    )
    return (grads.reshape(count, 2, size, size), jnp.sum(terms, axis=0))


def extract(tile, corners, size):
    zero = jnp.zeros((), jnp.int32)
    windows = jax.vmap(lambda row, col: lax.dynamic_slice(tile, (zero, row, col), (2, size, size)))(
        corners[:, 0], corners[:, 1]
    )
    return windows.astype(jnp.bfloat16)


def add_scaled(start_value, grads, corners, size):
    zero = jnp.zeros((), jnp.int32)

    def add_one(item, acc):
        corner = (zero, corners[item, 0], corners[item, 1])
        window = lax.dynamic_slice(acc, corner, (2, size, size))
        return lax.dynamic_update_slice(
            acc, window - 0.25 * grads[item].astype(jnp.float32), corner
        )

    return lax.fori_loop(0, grads.shape[0], add_one, start_value)


def shards(object_field, probe, amplitude, row_offset, col_offset, owner):
    n_pos = lax.axis_size("pos")
    n_obj = lax.axis_size("obj")
    pos_dev = amplitude.shape[0]
    size = amplitude.shape[1]
    capacity = max(2, pos_dev // n_pos + 1)
    slots = n_pos * capacity
    padded = padded_2(object_field.astype(jnp.bfloat16), (("pos", 2), ("obj", 1)), 1).astype(
        object_field.dtype
    )
    smooth = 4.0 * object_field - padded[:, :-2, 1:-1] - padded[:, 2:, 1:-1]
    smooth = smooth - padded[:, 1:-1, :-2] - padded[:, 1:-1, 2:]
    four_re, four_im = dft_tables(size)
    tables = (four_re, four_im, -four_im)
    onehot = (owner[:, None] == jnp.arange(n_pos, dtype=jnp.int32)[None, :]).astype(jnp.int32)
    earlier = jnp.cumsum(onehot, axis=0) - onehot
    ranking = jnp.sum(earlier * onehot, axis=1)
    target = owner * capacity + ranking
    matching = (target[:, None] == jnp.arange(slots, dtype=jnp.int32)[None, :]).astype(jnp.int32)
    source = jnp.sum(matching * jnp.arange(pos_dev, dtype=jnp.int32)[:, None], axis=0)
    filled = jnp.sum(matching, axis=0) > 0
    listing = jnp.stack([row_offset, col_offset, jnp.ones_like(row_offset)], axis=1)
    slot_info = jnp.where(filled[:, None], listing[source], 0).reshape(n_pos, capacity, 3)
    received = lax.all_to_all(slot_info, "pos", split_axis=0, concat_axis=0, tiled=True)
    items = received.shape[1]
    windows = extract(object_field, received.reshape(-1, 3), size)
    windows = windows.reshape(n_pos, items, 2, size, size)
    fetched = lax.all_to_all(windows, "pos", split_axis=0, concat_axis=0, tiled=True)
    mine = fetched.reshape(slots, 2, size, size)[target]
    grads, probe_part = run_terms(mine, amplitude, jnp.ones((pos_dev,), jnp.float32), probe, tables)
    grad_slots = jnp.where(filled[:, None, None, None], grads[source], jnp.zeros((), jnp.bfloat16))
    incoming = lax.all_to_all(
        grad_slots.reshape(n_pos, capacity, 2, size, size),
        "pos",
        split_axis=0,
        concat_axis=0,
        tiled=True,
    )
    incoming = incoming.reshape(slots, 2, size, size)
    corners = received.reshape(slots, 3)
    base = object_field - 0.125 * smooth
    new_object = add_scaled(base, incoming, corners, size)
    probe_grad = lax.psum(probe_part, ("pos", "obj"))
    n_total = pos_dev * n_pos * n_obj
    new_probe = probe - probe_grad * (1.0 / math.sqrt(n_total))
    return (new_object, new_probe)


def solution(mesh):
    placed = (
        P(None, "obj", "pos"),
        P(),
        P(("pos", "obj"), None, None),
        P(("pos", "obj")),
        P(("pos", "obj")),
        P(("pos", "obj")),
    )
    return jax.shard_map(
        shards, mesh=mesh, in_specs=placed, out_specs=(P(None, "obj", "pos"), P()), check_vma=False
    )
```

profile of v0, /device:TPU:15, one launch (start us, length us, event | category | flops | bytes accessed | tf_op | source)
XLA Modules:
  0.0 1008.5 jit_solution(17226852778361089383)
XLA Ops:
  12.1 6.8 all-to-all-start
  22.9 89.1 %while.29 = (s32[]{:T(128)}, bf16[2,512,384]{2,1,0:T(8,128)(2,1)S(1)}, s32[32,3]{0,1:T(4,128)S(1)}, bf16[32,2,256,256]{3,2,1,0:T(8,128)(2,1)}, s32[]{:T(128)}) while((s32[]{:T(128)}, bf16[2,512,384]{2,1,0:T(8,128)(2,1)S(1)}, s32[32,3]{0,1:T(4,128)S(1)}, bf16[32,2,256,256]{3,2,1,0:T(8,128)(2,1)}, s32[]{:T(128)}) %tuple.89), condition=%wide.while_cond, body=%wide.while_body.sunk | while | flops 2 | bytes 525929 | solution.py:101
  112.9 7.2 all-to-all-start.1
  120.1 130.6 %all-to-all-done.1 = bf16[16,2,2,256,256]{4,3,2,1,0:T(8,128)(2,1)} async-done(((bf16[16,2,2,256,256]{4,3,2,1,0:T(8,128)(2,1)}), bf16[16,2,2,256,256]{4,3,2,1,0:T(8,128)(2,1)}, u32[]{:S(2)}, u32[]{:S(2)}) %all-to-all-start.1) | async-done | bytes 8388640 | tf_op jit(solution)/shard_map/all_to_all | solution.py:147
  256.9 60.2 %while.30 = (s32[]{:T(128)}, bf16[2,8,2,256,256]{4,3,2,1,0:T(8,128)(2,1)}, f32[2,2,256,256]{3,2,1,0:T(8,128)S(1)}, f32[2,256,256]{2,1,0:T(8,128)S(1)}, bf16[2,8,...) while((s32[]{:T(128)}, ...), condition=%wide.region_7.8_spmd.clone.clone, body=%wide.region_4.7_spmd.clone.clone.sunk | while | flops 4348182528 | bytes 96470128 | solution.py:93
  317.1 7.5 gather_fusion.2
  324.6 7.2 broadcast_select_fusion
  331.8 9.4 all-to-all-start.2
  342.9 91.4 %collective-permute-done = bf16[2,512,1]{2,1,0:T(8,128)(2,1)S(1)} collective-permute-done((bf16[2,512,1]{2,1,0:T(8,128)(2,1)S(1)}, bf16[2,512,1]{2,1,0:T(8,128)(2,1)S(1)}, u32[]{:S(2)}, u32[]{:S(2)}) %collective-permute-start) | collective-permute-done | bytes 2080 | tf_op jit(solution)/shard_map/ppermute | solution.py:14
  435.7 11.3 %collective-permute-start.2 = (bf16[2,1,386]{2,1,0:T(2,128)(2,1)S(1)}, bf16[2,1,386]{2,1,0:T(2,128)(2,1)S(1)}, u32[]{:S(2)}, u32[]{:S(2)}) collective-permute-start(bf16[2,1,386]{2,1,0:T(2,128)(2,1)S(1)} %get-tuple-element.299), channel_id=1, source_target_pairs={{0,1},{1,2},{2,3},{3,4},{4,5},{5,6},{6,7},{7,0},{8,9},{9,10},{10,1... | collective-permute-start | bytes 4640 | tf_op jit(solution)/shard_map/ppermute | solution.py:14
  458.0 151.4 %all-reduce.2.cloned.1.call-done = f32[2,256,256]{2,1,0:T(8,128)} async-done(((f32[2,256,256]{2,1,0:T(8,128)}), f32[2,256,256]{2,1,0:T(8,128)}) %all-reduce.2.cloned.1.call-update) | async-done | bytes 524304 | tf_op jit(solution)/shard_map/psum | solution.py:162
  611.3 390.4 %while.28 = (s32[]{:T(128)}, f32[2,512,384]{2,1,0:T(8,128)}, s32[32,3]{0,1:T(4,128)S(1)}, bf16[32,2,256,256]{3,2,1,0:T(8,128)(2,1)}, s32[]{:T(128)}, /*index=5*/s32[]{:T(128)}, s32[]{:T(128)}, s32[]{:T(128)}) while((s32[]{:T(128)}, f32[2,512,384]{2,1,0:T(8,128)}, s32[32,3]{0,1:T(4,128)S(1)}, bf16[32,2,256,256]{3,2,1,0:T(8,128)(2,1)}, ...), condition=%wide.region_9.10_spmd, body=%wide.region_8.9_spmd.sunk | while | flops 393224 | bytes 2359485 | solution.py:117
  617.2 6.4 dynamic_update_slice.24
  641.4 6.5 dynamic_update_slice.24
  665.7 6.5 dynamic_update_slice.24
  678.0 6.5 dynamic_update_slice.24
  690.4 6.5 dynamic_update_slice.24
  702.7 6.5 dynamic_update_slice.24
  715.1 6.5 dynamic_update_slice.24
  727.5 6.4 dynamic_update_slice.24
  739.8 6.5 dynamic_update_slice.24
  752.1 6.3 dynamic_update_slice.24
  776.5 6.4 dynamic_update_slice.24
  788.7 6.4 dynamic_update_slice.24
  801.0 6.5 dynamic_update_slice.24
  825.3 6.4 dynamic_update_slice.24
  837.5 6.5 dynamic_update_slice.24
  885.8 6.4 dynamic_update_slice.24
  910.3 6.5 dynamic_update_slice.24
  946.8 6.5 dynamic_update_slice.24
  982.9 6.5 dynamic_update_slice.24
  995.3 6.4 dynamic_update_slice.24
  (274 shorter events, 321.1 us)
Async XLA Ops:
  12.1 10.6 %all-to-all-start = ((s32[16,2,3]{2,1,0:T(2,128)}), s32[16,2,3]{2,1,0:T(2,128)S(1)}, u32[]{:S(2)}, u32[]{:S(2)}) async-start(s32[16,2,3]{2,1,0:T(2,128)} %copy.88), calls=%async_computation | async-start | bytes 32768 | tf_op jit(solution)/shard_map/all_to_all | solution.py:143
  22.8 89.2 %copy-start.6 = (s32[32,3]{0,1:T(4,128)}, s32[32,3]{0,1:T(4,128)S(1)}, u32[]{:S(2)}) copy-start(s32[32,3]{0,1:T(4,128)S(1)} %copy.109) | copy-start | bytes 1156
  112.0 0.9 copy-start
  112.9 137.8 %all-to-all-start.1 = ((bf16[16,2,2,256,256]{4,3,2,1,0:T(8,128)(2,1)}), bf16[16,2,2,256,256]{4,3,2,1,0:T(8,128)(2,1)}, u32[]{:S(2)}, u32[]{:S(2)}) async-start(bf16[16,2,2,256,256]{4,3,2,1,0:T(8,128)(2,1)} %bitcast.241), calls=%async_computation.1 | async-start | bytes 16777216 | tf_op jit(solution)/shard_map/all_to_all | solution.py:147
  250.7 6.2 copy-start.2
  268.2 1.6 copy-start.8
  298.3 1.6 copy-start.8
  317.1 7.5 copy-start.3
  331.8 9.4 copy-start.1
  331.8 279.5 %all-to-all-start.2 = ((bf16[16,2,2,256,256]{4,3,2,1,0:T(8,128)(2,1)}), bf16[16,2,2,256,256]{4,3,2,1,0:T(8,128)(2,1)}, u32[]{:S(2)}, u32[]{:S(2)}) async-start(bf16[16,2,2,256,256]{4,3,2,1,0:T(8,128)(2,1)} %broadcast_select_fusion), calls=%async_computation.2 | async-start | bytes 16777216 | tf_op jit(solution)/shard_map/all_to_all | solution.py:151
  341.2 268.2 %all-reduce.2.cloned.1.call-start = ((), (), s32[]{:S(2)}) async-start(), calls=%async_computation.3 | async-start | bytes 1048576 | tf_op jit(solution)/shard_map/psum | solution.py:162
  341.4 92.9 %collective-permute-start = (bf16[2,512,1]{2,1,0:T(8,128)(2,1)S(1)}, bf16[2,512,1]{2,1,0:T(8,128)(2,1)S(1)}, u32[]{:S(2)}, u32[]{:S(2)}) collective-permute-start(bf16[2,512,1]{2,1,0:T(8,128)(2,1)S(1)} %get-tuple-element.301), channel_id=1, source_target_pairs={{0,8},{8,16},{16,24},{24,32},{32,40},{40,48},{48,56},{56,64},{64,7... | collective-permute-start | bytes 6152 | tf_op jit(solution)/shard_map/ppermute | solution.py:14
  342.6 91.7 %collective-permute-start.1 = (bf16[2,512,1]{2,1,0:T(8,128)(2,1)S(1)}, bf16[2,512,1]{2,1,0:T(8,128)(2,1)S(1)}, u32[]{:S(2)}, u32[]{:S(2)}) collective-permute-start(bf16[2,512,1]{2,1,0:T(8,128)(2,1)S(1)} %get-tuple-element.302), channel_id=1, source_target_pairs={{8,0},{16,8},{24,16},{32,24},{40,32},{48,40},{56,48},{64,56},{72,6... | collective-permute-start | bytes 6152 | tf_op jit(solution)/shard_map/ppermute | solution.py:17
  434.3 0.7 copy-start.4
  435.0 0.7 copy-start.5
  435.7 12.1 %collective-permute-start.2 = (bf16[2,1,386]{2,1,0:T(2,128)(2,1)S(1)}, bf16[2,1,386]{2,1,0:T(2,128)(2,1)S(1)}, u32[]{:S(2)}, u32[]{:S(2)}) collective-permute-start(bf16[2,1,386]{2,1,0:T(2,128)(2,1)S(1)} %get-tuple-element.299), channel_id=1, source_target_pairs={{0,1},{1,2},{2,3},{3,4},{4,5},{5,6},{6,7},{7,0},{8,9},{9,10},{10,1... | collective-permute-start | bytes 4640 | tf_op jit(solution)/shard_map/ppermute | solution.py:14
  447.1 3.0 collective-permute-start.3
  454.1 157.2 %copy-start.7 = (s32[32,3]{0,1:T(4,128)S(1)}, s32[32,3]{0,1:T(4,128)}, u32[]{:S(2)}) copy-start(s32[32,3]{0,1:T(4,128)} %copy-done.6) | copy-start | bytes 1156
Sparse Core Ops, SparseCore 0:
  454.2 155.1 all-reduce.1
where the time goes:
time: 1020 us; the launch traced here: 1010 us
  waiting for transfers between devices  379 us (37%)
  local copies, waits for them, and re-layouts  335 us (33%)
  loops' own time  122 us (12%)
  other arithmetic  70.1 us (7%)
  matrix products  53 us (5%)
  starting transfers between devices  36.3 us (4%)
  between operations  14.1 us (1%)
    dynamic_update_slice x32, local copies, waits for them, and re-layouts, add_one(): lax.dynamic_update_slice(acc, window - 0.25 * grads[item].astype(jnp.floa...  203 us
    psum x1, waiting for transfers between devices, shards(): probe_grad = lax.psum(probe_part, ('pos', 'obj'))  151 us
    all_to_all x1, waiting for transfers between devices, shards(): lax.all_to_all(windows, 'pos', split_axis=0, concat_axis=0, tiled=True)  131 us
    another operation x1, loops' own time, add_scaled(): return lax.fori_loop(0, grads.shape[0], add_one, start_value)  121 us
    ppermute x2, waiting for transfers between devices, padded_2(): lax.ppermute(lax.slice_in_dim(block, block.shape[dim] - width, None, axis...  92.1 us
    gather x96, local copies, waits for them, and re-layouts  89.1 us
    sub x32, other arithmetic, add_one(): window - 0.25 * grads[item].astype(jnp.float32)  45.3 us
    dot_general x16, matrix products, product(): jnp.einsum('bjk,kl->bjl', values, matrix, preferred_element_type=jnp.floa...  28.6 us
  transfers between devices with their start and end apart: 8, of which 6 were waited for; matrix products, arithmetic and copies ran while one was open for 1% of the time, Pallas kernels for 0%

commit v1 on v0

--- a/solution.py
+++ b/solution.py
@@ -159,7 +159,9 @@
     corners = received.reshape(slots, 3)
     base = object_field - 0.125 * smooth
     new_object = add_scaled(base, incoming, corners, size)
-    probe_grad = lax.psum(probe_part, ("pos", "obj"))
+    probe_grad = probe_part
+    for over in ("pos", "obj"):
+        probe_grad = lax.psum(probe_grad, over)
     n_total = pos_dev * n_pos * n_obj
     new_probe = probe - probe_grad * (1.0 / math.sqrt(n_total))
     return (new_object, new_probe)

time: 1020 us -> 970 us (0.951)
  waiting for transfers between devices: 379 us -> 339 us
    psum x1 -> x2, waiting for transfers between devices: 151 us -> 110 us  [shards(): probe_grad = lax.psum(probe_grad, over)]
  transfers between devices with their start and end apart: 8 -> 9, of which waited for: 6 -> 8; matrix products, arithmetic and copies ran while one was open for 1% -> 1% of each run, Pallas kernels for 0% -> 0%
where the time goes in v1:
time: 970 us; the launch traced here: 961 us
  waiting for transfers between devices  339 us (35%)
  local copies, waits for them, and re-layouts  334 us (34%)
  loops' own time  115 us (12%)
  other arithmetic  68.8 us (7%)
  matrix products  53 us (5%)
  starting transfers between devices  36.6 us (4%)
  between operations  14.1 us (1%)
    dynamic_update_slice x32, local copies, waits for them, and re-layouts, add_one(): lax.dynamic_update_slice(acc, window - 0.25 * grads[item].astype(jnp.floa...  203 us
    all_to_all x1, waiting for transfers between devices, shards(): lax.all_to_all(windows, 'pos', split_axis=0, concat_axis=0, tiled=True)  131 us
    another operation x1, loops' own time, add_scaled(): return lax.fori_loop(0, grads.shape[0], add_one, start_value)  114 us
    psum x2, waiting for transfers between devices, shards(): probe_grad = lax.psum(probe_grad, over)  110 us
    ppermute x2, waiting for transfers between devices, padded_2(): lax.ppermute(lax.slice_in_dim(block, block.shape[dim] - width, None, axis...  92.8 us
    gather x96, local copies, waits for them, and re-layouts  89.8 us
    sub x32, other arithmetic, add_one(): window - 0.25 * grads[item].astype(jnp.float32)  45.3 us
    dot_general x16, matrix products, product(): jnp.einsum('bjk,kl->bjl', values, matrix, preferred_element_type=jnp.floa...  28.6 us
  transfers between devices with their start and end apart: 9, of which 8 were waited for; matrix products, arithmetic and copies ran while one was open for 1% of the time, Pallas kernels for 0%

profile of v1, /device:TPU:15, one launch (start us, length us, event | category | flops | bytes accessed | tf_op | source)
XLA Modules:
  0.0 960.6 jit_solution(6573021338882997671)
XLA Ops:
  12.1 6.8 all-to-all-start
  22.9 89.9 %while.29 = (s32[]{:T(128)}, bf16[2,512,384]{2,1,0:T(8,128)(2,1)S(1)}, s32[32,3]{0,1:T(4,128)S(1)}, bf16[32,2,256,256]{3,2,1,0:T(8,128)(2,1)}, s32[]{:T(128)}) while((s32[]{:T(128)}, bf16[2,512,384]{2,1,0:T(8,128)(2,1)S(1)}, s32[32,3]{0,1:T(4,128)S(1)}, bf16[32,2,256,256]{3,2,1,0:T(8,128)(2,1)}, s32[]{:T(128)}) %tuple.89), condition=%wide.while_cond, body=%wide.while_body.sunk | while | flops 2 | bytes 525929 | solution.py:101
  113.6 7.2 all-to-all-start.1
  120.9 130.6 %all-to-all-done.1 = bf16[16,2,2,256,256]{4,3,2,1,0:T(8,128)(2,1)} async-done(((bf16[16,2,2,256,256]{4,3,2,1,0:T(8,128)(2,1)}), bf16[16,2,2,256,256]{4,3,2,1,0:T(8,128)(2,1)}, u32[]{:S(2)}, u32[]{:S(2)}) %all-to-all-start.1) | async-done | bytes 8388640 | tf_op jit(solution)/shard_map/all_to_all | solution.py:147
  257.7 60.2 %while.30 = (s32[]{:T(128)}, bf16[2,8,2,256,256]{4,3,2,1,0:T(8,128)(2,1)}, f32[2,2,256,256]{3,2,1,0:T(8,128)S(1)}, f32[2,256,256]{2,1,0:T(8,128)S(1)}, bf16[2,8,...) while((s32[]{:T(128)}, ...), condition=%wide.region_7.8_spmd.clone.clone, body=%wide.region_4.7_spmd.clone.clone.sunk | while | flops 4348182528 | bytes 96470128 | solution.py:93
  317.9 7.1 gather_fusion.2
  325.0 7.2 broadcast_select_fusion
  332.2 9.2 all-to-all-start.2
  344.4 92.0 %collective-permute-done = bf16[2,512,1]{2,1,0:T(8,128)(2,1)S(1)} collective-permute-done((bf16[2,512,1]{2,1,0:T(8,128)(2,1)S(1)}, bf16[2,512,1]{2,1,0:T(8,128)(2,1)S(1)}, u32[]{:S(2)}, u32[]{:S(2)}) %collective-permute-start) | collective-permute-done | bytes 2080 | tf_op jit(solution)/shard_map/ppermute | solution.py:14
  437.8 11.7 %collective-permute-start.2 = (bf16[2,1,386]{2,1,0:T(2,128)(2,1)S(1)}, bf16[2,1,386]{2,1,0:T(2,128)(2,1)S(1)}, u32[]{:S(2)}, u32[]{:S(2)}) collective-permute-start(bf16[2,1,386]{2,1,0:T(2,128)(2,1)S(1)} %get-tuple-element.299), channel_id=1, source_target_pairs={{0,1},{1,2},{2,3},{3,4},{4,5},{5,6},{6,7},{7,0},{8,9},{9,10},{10,1... | collective-permute-start | bytes 4640 | tf_op jit(solution)/shard_map/ppermute | solution.py:14
  454.7 50.1 %all-reduce.3.cloned.1.call-done = f32[2,256,256]{2,1,0:T(8,128)} async-done(((f32[2,256,256]{2,1,0:T(8,128)}), f32[2,256,256]{2,1,0:T(8,128)}) %all-reduce.3.cloned.1.call-update) | async-done | bytes 524304 | tf_op jit(solution)/shard_map/psum | solution.py:164
  508.8 60.3 %all-reduce.5.cloned.1.call-done = f32[2,256,256]{2,1,0:T(8,128)} async-done(((f32[2,256,256]{2,1,0:T(8,128)}), f32[2,256,256]{2,1,0:T(8,128)}) %all-reduce.5.cloned.1.call-update) | async-done | bytes 524304 | tf_op jit(solution)/shard_map/psum | solution.py:164
  571.0 382.8 %while.28 = (s32[]{:T(128)}, f32[2,512,384]{2,1,0:T(8,128)}, s32[32,3]{0,1:T(4,128)S(1)}, bf16[32,2,256,256]{3,2,1,0:T(8,128)(2,1)}, s32[]{:T(128)}, /*index=5*/s32[]{:T(128)}, s32[]{:T(128)}, s32[]{:T(128)}) while((s32[]{:T(128)}, f32[2,512,384]{2,1,0:T(8,128)}, s32[32,3]{0,1:T(4,128)S(1)}, bf16[32,2,256,256]{3,2,1,0:T(8,128)(2,1)}, ...), condition=%wide.region_9.10_spmd, body=%wide.region_8.9_spmd.sunk | while | flops 393224 | bytes 2359485 | solution.py:117
  576.6 6.4 dynamic_update_slice.24
  600.4 6.5 dynamic_update_slice.24
  624.2 6.5 dynamic_update_slice.24
  636.3 6.5 dynamic_update_slice.24
  648.4 6.5 dynamic_update_slice.24
  660.5 6.5 dynamic_update_slice.24
  672.7 6.5 dynamic_update_slice.24
  684.8 6.4 dynamic_update_slice.24
  696.9 6.5 dynamic_update_slice.24
  732.9 6.4 dynamic_update_slice.24
  744.9 6.4 dynamic_update_slice.24
  756.9 6.5 dynamic_update_slice.24
  780.7 6.4 dynamic_update_slice.24
  792.7 6.5 dynamic_update_slice.24
  840.1 6.4 dynamic_update_slice.24
  864.0 6.5 dynamic_update_slice.24
  899.8 6.5 dynamic_update_slice.24
  935.3 6.5 dynamic_update_slice.24
  947.4 6.4 dynamic_update_slice.24
  (275 shorter events, 326.8 us)
Async XLA Ops:
  12.1 10.6 %all-to-all-start = ((s32[16,2,3]{2,1,0:T(2,128)}), s32[16,2,3]{2,1,0:T(2,128)S(1)}, u32[]{:S(2)}, u32[]{:S(2)}) async-start(s32[16,2,3]{2,1,0:T(2,128)} %copy.88), calls=%async_computation | async-start | bytes 32768 | tf_op jit(solution)/shard_map/all_to_all | solution.py:143
  22.8 90.0 %copy-start.5 = (s32[32,3]{0,1:T(4,128)}, s32[32,3]{0,1:T(4,128)S(1)}, u32[]{:S(2)}) copy-start(s32[32,3]{0,1:T(4,128)S(1)} %copy.109) | copy-start | bytes 1156
  112.8 0.9 copy-start
  113.6 137.8 %all-to-all-start.1 = ((bf16[16,2,2,256,256]{4,3,2,1,0:T(8,128)(2,1)}), bf16[16,2,2,256,256]{4,3,2,1,0:T(8,128)(2,1)}, u32[]{:S(2)}, u32[]{:S(2)}) async-start(bf16[16,2,2,256,256]{4,3,2,1,0:T(8,128)(2,1)} %bitcast.241), calls=%async_computation.1 | async-start | bytes 16777216 | tf_op jit(solution)/shard_map/all_to_all | solution.py:147
  251.5 6.2 copy-start.2
  268.9 1.6 copy-start.7
  299.0 1.6 copy-start.7
  332.2 238.8 %all-to-all-start.2 = ((bf16[16,2,2,256,256]{4,3,2,1,0:T(8,128)(2,1)}), bf16[16,2,2,256,256]{4,3,2,1,0:T(8,128)(2,1)}, u32[]{:S(2)}, u32[]{:S(2)}) async-start(bf16[16,2,2,256,256]{4,3,2,1,0:T(8,128)(2,1)} %broadcast_select_fusion), calls=%async_computation.2 | async-start | bytes 16777216 | tf_op jit(solution)/shard_map/all_to_all | solution.py:151
  341.5 1.3 copy-start.1
  341.5 163.4 %all-reduce.3.cloned.1.call-start = ((), (), s32[]{:S(2)}) async-start(), calls=%async_computation.3 | async-start | bytes 1048576 | tf_op jit(solution)/shard_map/psum | solution.py:164
  342.4 226.6 %all-reduce.5.cloned.1.call-start = ((), (), s32[]{:S(2)}) async-start(), calls=%async_computation.4 | async-start | bytes 1048576 | tf_op jit(solution)/shard_map/psum | solution.py:164
  342.9 93.6 %collective-permute-start = (bf16[2,512,1]{2,1,0:T(8,128)(2,1)S(1)}, bf16[2,512,1]{2,1,0:T(8,128)(2,1)S(1)}, u32[]{:S(2)}, u32[]{:S(2)}) collective-permute-start(bf16[2,512,1]{2,1,0:T(8,128)(2,1)S(1)} %get-tuple-element.301), channel_id=1, source_target_pairs={{0,8},{8,16},{16,24},{24,32},{32,40},{40,48},{48,56},{56,64},{64,7... | collective-permute-start | bytes 6152 | tf_op jit(solution)/shard_map/ppermute | solution.py:14
  344.1 92.4 %collective-permute-start.1 = (bf16[2,512,1]{2,1,0:T(8,128)(2,1)S(1)}, bf16[2,512,1]{2,1,0:T(8,128)(2,1)S(1)}, u32[]{:S(2)}, u32[]{:S(2)}) collective-permute-start(bf16[2,512,1]{2,1,0:T(8,128)(2,1)S(1)} %get-tuple-element.302), channel_id=1, source_target_pairs={{8,0},{16,8},{24,16},{32,24},{40,32},{48,40},{56,48},{64,56},{72,6... | collective-permute-start | bytes 6152 | tf_op jit(solution)/shard_map/ppermute | solution.py:17
  436.4 0.7 copy-start.3
  437.1 0.7 copy-start.4
  437.8 12.5 %collective-permute-start.2 = (bf16[2,1,386]{2,1,0:T(2,128)(2,1)S(1)}, bf16[2,1,386]{2,1,0:T(2,128)(2,1)S(1)}, u32[]{:S(2)}, u32[]{:S(2)}) collective-permute-start(bf16[2,1,386]{2,1,0:T(2,128)(2,1)S(1)} %get-tuple-element.299), channel_id=1, source_target_pairs={{0,1},{1,2},{2,3},{3,4},{4,5},{5,6},{6,7},{7,0},{8,9},{9,10},{10,1... | collective-permute-start | bytes 4640 | tf_op jit(solution)/shard_map/ppermute | solution.py:14
  449.6 3.3 collective-permute-start.3
  504.9 66.1 %copy-start.6 = (s32[32,3]{0,1:T(4,128)S(1)}, s32[32,3]{0,1:T(4,128)}, u32[]{:S(2)}) copy-start(s32[32,3]{0,1:T(4,128)} %copy-done.5) | copy-start | bytes 1156
Sparse Core Ops, SparseCore 0:
  346.1 158.7 all-reduce.2
  507.3 61.7 all-reduce.4
